TPU v7x, 256 devices: a whole 4x4x8 slice. The times are simulated.
256 devices in a mesh: seq: 32 (over y, x, core), grp: 8 (over z).
Axes of the slice: x: 4, y: 4, z: 8, core: 2. Of those that a mesh axis runs over, the one named last changes fastest.
Arguments:
- hidden_in: bfloat16 [98304, 2048], P(('grp', 'seq')), parts along dimension 0, may hold values from -8 to 8
- norm_gain: bfloat16 [2048], replicated, may hold values from 0.099609375 to 1.8984375
- w_query: bfloat16 [2048, 2048], P('seq'), may hold values from -1 to 1
- w_key: bfloat16 [2048, 128], P('seq'), may hold values from -1 to 1
- w_value: bfloat16 [2048, 128], P('seq'), may hold values from -0.125 to 0.125
- w_out: bfloat16 [2048, 2048], P('seq'), may hold values from -0.625 to 0.625
- seg_ids: int32 [98304], P('grp'), parts along dimension 0, may hold values from 0 to 1, never falling along the last dimension, each value on 1 to 11904 neighbouring positions
- cache_slot: int32 [768], P('grp'), parts along dimension 0, may hold values from 0 to 95, each once
Outputs:
- hidden_out: bfloat16 [98304, 2048], P(('grp', 'seq')), parts along dimension 0
- kv_cache: bfloat16 [98304, 256], P(('grp', 'seq')), parts along dimension 0
There are 8 independent parts, one for each index of `grp`. A program takes and returns all parts, laid end to end along the dimension named above; an argument that names none is the same for every part. Nothing has to cross between parts.
Inputs may be any that keep to these rules, and one draw needn't show every extreme that they name: `seg_ids`: segment numbers never fall along the stream; each prompt holds 1 to 11904 tokens. `cache_slot`: every cache position appears exactly once.
All inputs are finite; a program needn't handle non-finite values.
Results may differ from a plain program's by a relative error of at most 0.01.
Values may be sent and summed in bfloat16 or wider, within the bound.
No kernel may reach another device: no remote copies, remote signals or barrier semaphores. Data moves between devices by JAX's collectives and lax.ppermute only.
A program may use at most 256 MiB of HBM per device.

v0:
```python
import jax
import jax.numpy as jnp
from jax import lax
from jax.sharding import PartitionSpec as P

WINDOW = 1024
CACHE_BLK = 128
REACH = 3
EPSILON = 1e-06


def shifted(array, axis, by):
    length = lax.axis_size(axis)
    pairs = [(i, i + by) for i in range(length) if 0 <= i + by < length]
    return lax.ppermute(array, axis, pairs)


def normalize(hidden_in, norm_gain):
    values_wide = hidden_in.astype(jnp.float32)
    mean_square = jnp.mean(values_wide * values_wide, axis=1, keepdims=True)
    return (values_wide * lax.rsqrt(mean_square + EPSILON) * norm_gain.astype(jnp.float32)).astype(
        jnp.bfloat16
    )


def attend_block(queries, key_rows, value_rows, seg_query, seg_key, pos_query, pos_key):
    row_count = queries.shape[0]
    head_dim = key_rows.shape[1]
    head_count = queries.shape[1] // head_dim
    visible = (
        (seg_query[:, None] == seg_key[None, :])
        & (pos_key[None, :] <= pos_query[:, None])
        & (pos_key[None, :] > pos_query[:, None] - WINDOW)
    )
    score_scale = 1.0 / head_dim**0.5

    def one_head(query_head):
        scores = (
            lax.dot_general(
                query_head, key_rows, (((1,), (1,)), ((), ())), preferred_element_type=jnp.float32
            )
            * score_scale
        )
        scores = jnp.where(visible, scores, -jnp.inf)
        row_top = jnp.max(scores, axis=1, keepdims=True)
        weights = jnp.exp(scores - row_top).astype(jnp.bfloat16)
        weight_sum = jnp.sum(weights.astype(jnp.float32), axis=1, keepdims=True)
        mixture = jnp.dot(weights, value_rows, preferred_element_type=jnp.float32) / weight_sum
        return mixture.astype(jnp.bfloat16)

    per_head = jnp.transpose(queries.reshape(row_count, head_count, head_dim), (1, 0, 2))
    result = lax.map(one_head, per_head)
    return jnp.transpose(result, (1, 0, 2)).reshape(row_count, head_count * head_dim)


def shards(hidden_in, norm_gain, w_query, w_key, w_value, w_out, seg_ids, cache_slot):
    row_count = hidden_in.shape[0]
    devices = lax.axis_size("seq")
    my_index = lax.axis_index("seq")
    normed = normalize(hidden_in, norm_gain)
    head_dim = w_key.shape[1]
    pieces = (
        lax.all_gather(w_query, "seq", axis=0, tiled=True),
        lax.all_gather(w_key, "seq", axis=0, tiled=True),
        lax.all_gather(w_value, "seq", axis=0, tiled=True),
    )
    columns = normed
    query_sum, key_sum, value_sum = tuple(
        (jnp.dot(columns, piece, preferred_element_type=jnp.float32) for piece in pieces)
    )
    query = query_sum.astype(jnp.bfloat16)
    stacked = jnp.concatenate(
        [key_sum.astype(jnp.bfloat16), value_sum.astype(jnp.bfloat16)], axis=1
    )
    margin = REACH * row_count
    span = (REACH + 1) * row_count
    reach_now = min(REACH, devices - 1)
    missing = jnp.zeros(((REACH - reach_now) * row_count, 2 * head_dim), jnp.bfloat16)
    received = []
    current = stacked
    for distance in range(reach_now):
        current = shifted(current, "seq", 1)
        received.append(current)
    window_rows = jnp.concatenate([missing] + received[::-1] + [stacked], axis=0)
    first_row = my_index * row_count
    seg_pad = jnp.concatenate([jnp.full((margin,), -1, jnp.int32), seg_ids])
    seg_query = lax.dynamic_slice_in_dim(seg_ids, first_row, row_count, 0)
    seg_key = lax.dynamic_slice_in_dim(seg_pad, first_row, span, 0)
    pos_query = first_row + jnp.arange(row_count, dtype=jnp.int32)
    pos_key = first_row - margin + jnp.arange(span, dtype=jnp.int32)
    attended = attend_block(
        query,
        window_rows[:, :head_dim],
        window_rows[:, head_dim:],
        seg_query,
        seg_key,
        pos_query,
        pos_key,
    )
    columns = attended
    projected = jnp.dot(
        columns,
        lax.all_gather(w_out, "seq", axis=0, tiled=True),
        preferred_element_type=jnp.float32,
    )
    hidden_out = (hidden_in.astype(jnp.float32) + projected).astype(jnp.bfloat16)
    blocks_per_dev = row_count // CACHE_BLK
    block_total = cache_slot.shape[0]
    slot_ids = jnp.arange(block_total, dtype=jnp.int32)
    source_of = jnp.sum(
        jnp.where(cache_slot[None, :] == slot_ids[:, None], slot_ids[None, :], 0), axis=1
    )
    owned_sources = lax.dynamic_slice_in_dim(
        source_of, my_index * blocks_per_dev, blocks_per_dev, 0
    )
    within = jnp.arange(row_count, dtype=jnp.int32)
    source_row = (
        jnp.repeat(owned_sources, CACHE_BLK, total_repeat_length=row_count) * CACHE_BLK
        + within % CACHE_BLK
    )
    piece = lax.all_gather(stacked, "seq", axis=0, tiled=True)
    inside = (source_row >= 0) & (source_row < piece.shape[0])
    taken = jnp.take(piece, jnp.clip(source_row, 0, piece.shape[0] - 1), axis=0)
    kv_cache = jnp.where(inside[:, None], taken, jnp.zeros_like(stacked))
    return (hidden_out, kv_cache)


def solution(mesh):
    in_specs = (
        P(("grp", "seq"), None),
        P(),
        P("seq", None),
        P("seq", None),
        P("seq", None),
        P("seq", None),
        P("grp"),
        P("grp"),
    )
    out_specs = (P(("grp", "seq"), None), P(("grp", "seq"), None))
    return jax.shard_map(shards, mesh=mesh, in_specs=in_specs, out_specs=out_specs, check_vma=False)
```

profile of v0, /device:TPU:1, one launch (start us, length us, event | category | flops | bytes accessed | tf_op | source)
XLA Modules:
  0.0 271.4 jit_solution(2322478954140555485)
XLA Ops:
  9.8 26.4 %all_gather.17 = bf16[2048,128]{1,0:T(8,128)(2,1)S(1)} all-gather(bf16[64,128]{1,0:T(8,128)(2,1)} %param.16), channel_id=1, replica_groups=mesh['seq'=32,'grp'=8] {'seq'}, dimensions={0}, use_global_device_ids=true | all-gather | bytes 540672 | tf_op jit(solution)/shard_map/all_gather | solution.py:65
  36.3 24.1 %all_gather.16 = bf16[2048,128]{1,0:T(8,128)(2,1)S(1)} all-gather(bf16[64,128]{1,0:T(8,128)(2,1)} %param.15), channel_id=1, replica_groups=mesh['seq'=32,'grp'=8] {'seq'}, dimensions={0}, use_global_device_ids=true | all-gather | bytes 540672 | tf_op jit(solution)/shard_map/all_gather | solution.py:64
  63.4 1.9 collective-permute-start
  66.3 2.0 fusion.23
  68.4 4.1 %collective-permute-start.1 = (bf16[384,256]{0,1:T(8,128)(2,1)S(1)}, bf16[384,256]{0,1:T(8,128)(2,1)S(1)}, u32[]{:S(2)}, u32[]{:S(2)}) collective-permute-start(bf16[384,256]{0,1:T(8,128)(2,1)S(1)} %collective-permute-done), channel_id=1, source_target_pairs={{0,8},{8,16},{16,24},{24,32},{32,40},{40,48},{48,56},{56,64},{64,7... | collective-permute-start | bytes 589832 | tf_op jit(solution)/shard_map/ppermute | solution.py:15
  72.5 2.6 collective-permute-done.1
  75.1 4.6 %collective-permute-start.2 = (bf16[384,256]{0,1:T(8,128)(2,1)S(1)}, bf16[384,256]{0,1:T(8,128)(2,1)S(1)}, u32[]{:S(2)}, u32[]{:S(2)}) collective-permute-start(bf16[384,256]{0,1:T(8,128)(2,1)S(1)} %collective-permute-done.1), channel_id=1, source_target_pairs={{0,8},{8,16},{16,24},{24,32},{32,40},{40,48},{48,56},{56,64},{64,7... | collective-permute-start | bytes 589832 | tf_op jit(solution)/shard_map/ppermute | solution.py:15
  79.7 3.3 %collective-permute-done.2 = bf16[384,256]{0,1:T(8,128)(2,1)S(1)} collective-permute-done((bf16[384,256]{0,1:T(8,128)(2,1)S(1)}, bf16[384,256]{0,1:T(8,128)(2,1)S(1)}, u32[]{:S(2)}, u32[]{:S(2)}) %collective-permute-start.2) | collective-permute-done | bytes 196640 | tf_op jit(solution)/shard_map/ppermute | solution.py:15
  84.9 37.7 %all-gather.8.cloned.1.call-done = bf16[12288,256]{0,1:T(8,128)(2,1)} async-done(((bf16[384,256]{0,1:T(8,128)(2,1)}), bf16[12288,256]{0,1:T(8,128)(2,1)}) %all-gather.8.cloned.1.call-update) | async-done | bytes 6291472 | tf_op jit(solution)/shard_map/all_gather | solution.py:121
  122.7 8.6 %copy.23 = bf16[12288,256]{1,0:T(8,128)(2,1)} copy(bf16[12288,256]{0,1:T(8,128)(2,1)} %all-gather.8.cloned.1.call-done) | data formatting | bytes 12582912 | tf_op jit(solution)/shard_map/all_gather | solution.py:121
  131.3 5.3 %gather_fusion = bf16[384,256]{1,0:T(8,128)(2,1)S(1)} fusion(bf16[12288,256]{1,0:T(8,128)(2,1)} %copy.23, s32[1024]{0:T(1024)S(1)} %pad_clamp_fusion), kind=kCustom, calls=%fused_computation | custom fusion | bytes 394752 | tf_op jit(solution)/shard_map/jit(_take)/gather | solution.py:123
  137.4 45.4 %all-gather.4.cloned.1.call-done = bf16[2048,2048]{1,0:T(8,128)(2,1)} async-done(((bf16[64,2048]{1,0:T(8,128)(2,1)}), bf16[2048,2048]{1,0:T(8,128)(2,1)}) %all-gather.4.cloned.1.call-update) | async-done | bytes 8388624 | tf_op jit(solution)/shard_map/all_gather | solution.py:63
  182.8 6.8 %fusion.12 = bf16[48,16,8,128]{3,2,1,0:T(8,128)(2,1)S(1)} fusion(bf16[2048,2048]{1,0:T(8,128)(2,1)} %all-gather.4.cloned.1.call-done, bf16[384,2048]{1,0:T(8,128)(2,1)S(1)} %copy-done, f32[2048]{0:T(1024)S(1)} %convert_element_type.32, f32[384]{0:T(512)S(1)} %add_rsqrt_fusion), kind=kOutput, calls=%fused_computation.22 | convolution fusion | flops 3225157632 | bytes 11544064 | tf_op jit(solution)/shard_map/dot_general | solution.py:69
  190.1 66.2 %while.12 = (s32[]{:T(128)}, bf16[16,384,128]{1,2,0:T(8,128)(2,1)}, bf16[16,384,128]{2,1,0:T(8,128)(2,1)S(1)}, bf16[1536,128]{1,0:T(8,128)(2,1)}, bf16[1536,128]...) while((s32[]{:T(128)}, bf16[16,384,128]{1,2,0:T(8,128)(2,1)}, ...), condition=%wide.region_4.5_spmd.clone, body=%wide.region_1.4_spmd.clone.sunk | while | flops 309165312 | bytes 10055833 | solution.py:52
  194.2 1.9 fusion.47
  206.6 1.9 fusion.47
  214.9 1.9 fusion.47
  219.0 1.9 fusion.47
  223.2 1.9 fusion.47
  227.3 1.9 fusion.47
  231.5 1.9 fusion.47
  235.6 1.9 fusion.47
  239.8 1.9 fusion.47
  256.3 8.5 %fusion.11 = bf16[384,2048]{1,0:T(8,128)(2,1)} fusion(bf16[384,2048]{1,0:T(8,128)(2,1)S(1)} %copy-done, bf16[384,2048]{0,1:T(8,128)(2,1)} %bitcast.62, bf16[2048,2048]{1,0:T(8,128)(2,1)} %all-gather.6.cloned.1.call-done), kind=kOutput, calls=%fused_computation.19 | convolution fusion | flops 3223584768 | bytes 13107200 | tf_op jit(solution)/shard_map/dot_general | solution.py:101
  (140 shorter events, 58.9 us)
Async XLA Ops:
  7.2 53.2 %copy-start = (bf16[384,2048]{1,0:T(8,128)(2,1)S(1)}, bf16[384,2048]{1,0:T(8,128)(2,1)}, u32[]{:S(2)}) copy-start(bf16[384,2048]{1,0:T(8,128)(2,1)} %param.12) | copy-start | bytes 4718596
  7.2 115.5 %all-gather.8.cloned.1.call-start = ((), (), s32[]{:S(2)}) async-start(), calls=%async_computation.2 | async-start | bytes 6488064 | tf_op jit(solution)/shard_map/all_gather | solution.py:121
  61.1 4.3 %copy-start.3 = (s32[96]{0:T(128)S(1)}, s32[96]{0:T(128)}, u32[]{:S(2)}) copy-start(s32[96]{0:T(128)} %param.19) | copy-start | bytes 1156
  61.1 5.1 %copy-start.2 = (s32[12288]{0:T(1024)S(1)}, s32[12288]{0:T(1024)}, u32[]{:S(2)}) copy-start(s32[12288]{0:T(1024)} %param.18) | copy-start | bytes 147460
  62.6 120.3 %all-gather.4.cloned.1.call-start = ((), (), s32[]{:S(2)}) async-start(), calls=%async_computation | async-start | bytes 8650752 | tf_op jit(solution)/shard_map/all_gather | solution.py:63
  63.3 193.0 %all-gather.6.cloned.1.call-start = ((), (), s32[]{:S(2)}) async-start(), calls=%async_computation.1 | async-start | bytes 8650752 | tf_op jit(solution)/shard_map/all_gather | solution.py:103
  63.4 5.0 %collective-permute-start = (bf16[384,256]{0,1:T(8,128)(2,1)}, bf16[384,256]{0,1:T(8,128)(2,1)S(1)}, u32[]{:S(2)}, u32[]{:S(2)}) collective-permute-start(bf16[384,256]{0,1:T(8,128)(2,1)} %pad_maximum_fusion), channel_id=1, source_target_pairs={{0,8},{8,16},{16,24},{24,32},{32,40},{40,48},{48,56},{56,64},{64,7... | collective-permute-start | bytes 589832 | tf_op jit(solution)/shard_map/ppermute | solution.py:15
  68.4 6.7 %collective-permute-start.1 = (bf16[384,256]{0,1:T(8,128)(2,1)S(1)}, bf16[384,256]{0,1:T(8,128)(2,1)S(1)}, u32[]{:S(2)}, u32[]{:S(2)}) collective-permute-start(bf16[384,256]{0,1:T(8,128)(2,1)S(1)} %collective-permute-done), channel_id=1, source_target_pairs={{0,8},{8,16},{16,24},{24,32},{32,40},{40,48},{48,56},{56,64},{64,7... | collective-permute-start | bytes 589832 | tf_op jit(solution)/shard_map/ppermute | solution.py:15
  75.1 7.9 %collective-permute-start.2 = (bf16[384,256]{0,1:T(8,128)(2,1)S(1)}, bf16[384,256]{0,1:T(8,128)(2,1)S(1)}, u32[]{:S(2)}, u32[]{:S(2)}) collective-permute-start(bf16[384,256]{0,1:T(8,128)(2,1)S(1)} %collective-permute-done.1), channel_id=1, source_target_pairs={{0,8},{8,16},{16,24},{24,32},{32,40},{40,48},{48,56},{56,64},{64,7... | collective-permute-start | bytes 589832 | tf_op jit(solution)/shard_map/ppermute | solution.py:15
  192.0 1.0 copy-start.1
  196.1 1.0 copy-start.1
  200.2 1.0 copy-start.1
  204.4 1.0 copy-start.1
  212.6 1.0 copy-start.1
  216.7 1.0 copy-start.1
  220.9 1.0 copy-start.1
  225.1 1.0 copy-start.1
  229.2 1.0 copy-start.1
  233.4 1.0 copy-start.1
  237.5 1.0 copy-start.1
  241.7 1.0 copy-start.1
  245.8 1.0 copy-start.1
  249.9 1.0 copy-start.1
  254.1 1.0 copy-start.1
  (1 other events, 1.0 us)
Sparse Core Ops, SparseCore 0:
  62.7 59.9 all-gather.7
  125.2 57.5 all-gather.3
  185.4 57.5 all-gather.5
where the time goes:
time: 273 us; the launch traced here: 271 us
  waiting for transfers between devices  89.7 us (33%)
  matrix products  54.3 us (20%)
  blocking collectives  50.5 us (18%)
  local copies, waits for them, and re-layouts  37.7 us (14%)
  other arithmetic  14.3 us (5%)
  between operations  13.9 us (5%)
  starting transfers between devices  10.7 us (4%)
    all_gather x1, waiting for transfers between devices, shards(): lax.all_gather(w_query, 'seq', axis=0, tiled=True)  45.4 us
    all_gather x1, waiting for transfers between devices, shards(): piece = lax.all_gather(stacked, 'seq', axis=0, tiled=True)  37.7 us
    dot_general x16, matrix products, one_head(): lax.dot_general(query_head, key_rows, (((1,), (1,)), ((), ())), preferred...  30 us
    all_gather x1, blocking collectives, shards(): lax.all_gather(w_value, 'seq', axis=0, tiled=True)  26.4 us
    all_gather x1, blocking collectives, shards(): lax.all_gather(w_key, 'seq', axis=0, tiled=True)  24.1 us
    dynamic_update_slice x32, local copies, waits for them, and re-layouts, attend_block(): result = lax.map(one_head, per_head)  12.5 us
    ppermute x3, starting transfers between devices, shifted(): return lax.ppermute(array, axis, pairs)  10.5 us
    all_gather x1, local copies, waits for them, and re-layouts, shards(): piece = lax.all_gather(stacked, 'seq', axis=0, tiled=True)  8.63 us
  transfers between devices with their start and end apart: 6, of which 4 were waited for; matrix products, arithmetic and copies ran while one was open for 31% of the time, Pallas kernels for 0%

commit v1 on v0

--- a/solution.py
+++ b/solution.py
@@ -7,6 +7,12 @@
 CACHE_BLK = 128
 REACH = 3
 EPSILON = 1e-06
+
+
+def gather_by_exchange(x, axis, dim):
+    devices = lax.axis_size(axis)
+    repeats = [devices if d == dim else 1 for d in range(x.ndim)]
+    return lax.all_to_all(jnp.tile(x, repeats), axis, split_axis=dim, concat_axis=dim, tiled=True)
 
 
 def shifted(array, axis, by):
@@ -62,7 +68,7 @@
     pieces = (
         lax.all_gather(w_query, "seq", axis=0, tiled=True),
         lax.all_gather(w_key, "seq", axis=0, tiled=True),
-        lax.all_gather(w_value, "seq", axis=0, tiled=True),
+        gather_by_exchange(w_value, "seq", 0),
     )
     columns = normed
     query_sum, key_sum, value_sum = tuple(

time: 273 us -> 258 us (0.945)
  blocking collectives: 50.5 us -> 27.6 us
  starting transfers between devices: 10.7 us -> 19.5 us
    all_gather x1 -> x0, blocking collectives: 26.4 us -> none  [shards(): lax.all_gather(w_value, 'seq', axis=0, tiled=True)]
    all_to_all x0 -> x1, starting transfers between devices: none -> 8.59 us  [gather_by_exchange(): lax.all_to_all(jnp.tile(x, repeats), axis, split_axis=dim, concat_axis=di...]
    all_gather x1, waiting for transfers between devices: 37.7 us -> 33.3 us  [shards(): piece = lax.all_gather(stacked, 'seq', axis=0, tiled=True)]
    ppermute x3, waiting for transfers between devices: 5.86 us -> 9.39 us  [shifted(): return lax.ppermute(array, axis, pairs)]
    all_gather x1, blocking collectives: 24.1 us -> 27.6 us  [shards(): lax.all_gather(w_key, 'seq', axis=0, tiled=True)]
  transfers between devices with their start and end apart: 6 -> 7, of which waited for: 4 -> 5; matrix products, arithmetic and copies ran while one was open for 31% -> 33% of each run, Pallas kernels for 0% -> 0%
where the time goes in v1:
time: 258 us; the launch traced here: 256 us
  waiting for transfers between devices  89.5 us (35%)
  matrix products  54.3 us (21%)
  local copies, waits for them, and re-layouts  39.3 us (15%)
  blocking collectives  27.6 us (11%)
  starting transfers between devices  19.5 us (8%)
  between operations  14 us (5%)
  other arithmetic  11.9 us (5%)
    all_gather x1, waiting for transfers between devices, shards(): lax.all_gather(w_query, 'seq', axis=0, tiled=True)  45.4 us
    all_gather x1, waiting for transfers between devices, shards(): piece = lax.all_gather(stacked, 'seq', axis=0, tiled=True)  33.3 us
    dot_general x16, matrix products, one_head(): lax.dot_general(query_head, key_rows, (((1,), (1,)), ((), ())), preferred...  30 us
    all_gather x1, blocking collectives, shards(): lax.all_gather(w_key, 'seq', axis=0, tiled=True)  27.6 us
    dynamic_update_slice x32, local copies, waits for them, and re-layouts, attend_block(): result = lax.map(one_head, per_head)  12.5 us
    ppermute x3, starting transfers between devices, shifted(): return lax.ppermute(array, axis, pairs)  10.7 us
    ppermute x3, waiting for transfers between devices, shifted(): return lax.ppermute(array, axis, pairs)  9.39 us
    all_gather x1, local copies, waits for them, and re-layouts, shards(): piece = lax.all_gather(stacked, 'seq', axis=0, tiled=True)  8.62 us
  transfers between devices with their start and end apart: 7, of which 5 were waited for; matrix products, arithmetic and copies ran while one was open for 33% of the time, Pallas kernels for 0%

profile of v1, /device:TPU:1, one launch (start us, length us, event | category | flops | bytes accessed | tf_op | source)
XLA Modules:
  0.0 256.3 jit_solution(11627310281379975193)
XLA Ops:
  8.9 8.6 %all-to-all-start = ((bf16[32,64,128]{2,1,0:T(8,128)(2,1)}), bf16[32,64,128]{2,1,0:T(8,128)(2,1)S(1)}, u32[]{:S(2)}, u32[]{:S(2)}) async-start(bf16[32,64,128]{2,1,0:T(8,128)(2,1)} %tile.2), calls=%async_computation | async-start | bytes 1048576 | tf_op jit(solution)/shard_map/all_to_all | solution.py:15
  18.0 27.6 %all_gather.13 = bf16[2048,128]{1,0:T(8,128)(2,1)S(1)} all-gather(bf16[64,128]{1,0:T(8,128)(2,1)S(1)} %copy-done.3), channel_id=1, replica_groups=mesh['seq'=32,'grp'=8] {'seq'}, dimensions={0}, use_global_device_ids=true | all-gather | bytes 540672 | tf_op jit(solution)/shard_map/all_gather | solution.py:70
  52.1 1.9 collective-permute-start
  54.1 2.8 %collective-permute-done = bf16[384,256]{0,1:T(8,128)(2,1)S(1)} collective-permute-done((bf16[384,256]{0,1:T(8,128)(2,1)}, bf16[384,256]{0,1:T(8,128)(2,1)S(1)}, u32[]{:S(2)}, u32[]{:S(2)}) %collective-permute-start) | collective-permute-done | bytes 196640 | tf_op jit(solution)/shard_map/ppermute | solution.py:21
  56.9 4.3 %collective-permute-start.1 = (bf16[384,256]{0,1:T(8,128)(2,1)S(1)}, bf16[384,256]{0,1:T(8,128)(2,1)S(1)}, u32[]{:S(2)}, u32[]{:S(2)}) collective-permute-start(bf16[384,256]{0,1:T(8,128)(2,1)S(1)} %collective-permute-done), channel_id=1, source_target_pairs={{0,8},{8,16},{16,24},{24,32},{32,40},{40,48},{48,56},{56,64},{64,7... | collective-permute-start | bytes 589832 | tf_op jit(solution)/shard_map/ppermute | solution.py:21
  61.2 3.1 %collective-permute-done.1 = bf16[384,256]{0,1:T(8,128)(2,1)S(1)} collective-permute-done((bf16[384,256]{0,1:T(8,128)(2,1)S(1)}, bf16[384,256]{0,1:T(8,128)(2,1)S(1)}, u32[]{:S(2)}, u32[]{:S(2)}) %collective-permute-start.1) | collective-permute-done | bytes 196640 | tf_op jit(solution)/shard_map/ppermute | solution.py:21
  64.3 4.6 %collective-permute-start.2 = (bf16[384,256]{0,1:T(8,128)(2,1)S(1)}, bf16[384,256]{0,1:T(8,128)(2,1)S(1)}, u32[]{:S(2)}, u32[]{:S(2)}) collective-permute-start(bf16[384,256]{0,1:T(8,128)(2,1)S(1)} %collective-permute-done.1), channel_id=1, source_target_pairs={{0,8},{8,16},{16,24},{24,32},{32,40},{40,48},{48,56},{56,64},{64,7... | collective-permute-start | bytes 589832 | tf_op jit(solution)/shard_map/ppermute | solution.py:21
  68.9 3.5 %collective-permute-done.2 = bf16[384,256]{0,1:T(8,128)(2,1)S(1)} collective-permute-done((bf16[384,256]{0,1:T(8,128)(2,1)S(1)}, bf16[384,256]{0,1:T(8,128)(2,1)S(1)}, u32[]{:S(2)}, u32[]{:S(2)}) %collective-permute-start.2) | collective-permute-done | bytes 196640 | tf_op jit(solution)/shard_map/ppermute | solution.py:21
  74.4 33.3 %all-gather.8.cloned.1.call-done = bf16[12288,256]{0,1:T(8,128)(2,1)} async-done(((bf16[384,256]{0,1:T(8,128)(2,1)}), bf16[12288,256]{0,1:T(8,128)(2,1)}) %all-gather.8.cloned.1.call-update) | async-done | bytes 6291472 | tf_op jit(solution)/shard_map/all_gather | solution.py:127
  107.7 8.6 %copy.23 = bf16[12288,256]{1,0:T(8,128)(2,1)} copy(bf16[12288,256]{0,1:T(8,128)(2,1)} %all-gather.8.cloned.1.call-done) | data formatting | bytes 12582912 | tf_op jit(solution)/shard_map/all_gather | solution.py:127
  116.3 5.3 %gather_fusion = bf16[384,256]{1,0:T(8,128)(2,1)S(1)} fusion(bf16[12288,256]{1,0:T(8,128)(2,1)} %copy.23, s32[1024]{0:T(1024)S(1)} %pad_clamp_fusion), kind=kCustom, calls=%fused_computation | custom fusion | bytes 394752 | tf_op jit(solution)/shard_map/jit(_take)/gather | solution.py:129
  122.4 45.4 %all-gather.4.cloned.1.call-done = bf16[2048,2048]{1,0:T(8,128)(2,1)} async-done(((bf16[64,2048]{1,0:T(8,128)(2,1)}), bf16[2048,2048]{1,0:T(8,128)(2,1)}) %all-gather.4.cloned.1.call-update) | async-done | bytes 8388624 | tf_op jit(solution)/shard_map/all_gather | solution.py:69
  167.8 6.8 %fusion.12 = bf16[48,16,8,128]{3,2,1,0:T(8,128)(2,1)S(1)} fusion(bf16[2048,2048]{1,0:T(8,128)(2,1)} %all-gather.4.cloned.1.call-done, bf16[384,2048]{1,0:T(8,128)(2,1)S(1)} %copy-done, f32[2048]{0:T(1024)S(1)} %convert_element_type.32, f32[384]{0:T(512)S(1)} %add_rsqrt_fusion), kind=kOutput, calls=%fused_computation.22 | convolution fusion | flops 3225157632 | bytes 11544064 | tf_op jit(solution)/shard_map/dot_general | solution.py:75
  175.1 66.2 %while.12 = (s32[]{:T(128)}, bf16[16,384,128]{1,2,0:T(8,128)(2,1)}, bf16[16,384,128]{2,1,0:T(8,128)(2,1)S(1)}, bf16[1536,128]{1,0:T(8,128)(2,1)}, bf16[1536,128]...) while((s32[]{:T(128)}, bf16[16,384,128]{1,2,0:T(8,128)(2,1)}, ...), condition=%wide.region_4.5_spmd.clone, body=%wide.region_1.4_spmd.clone.sunk | while | flops 309165312 | bytes 10055833 | solution.py:58
  175.1 1.9 fusion.47
  179.2 1.9 fusion.47
  191.6 1.9 fusion.47
  195.8 1.9 fusion.47
  208.2 1.9 fusion.47
  212.3 1.9 fusion.47
  216.4 1.9 fusion.47
  220.6 1.9 fusion.47
  224.8 1.9 fusion.47
  241.3 8.5 %fusion.11 = bf16[384,2048]{1,0:T(8,128)(2,1)} fusion(bf16[384,2048]{1,0:T(8,128)(2,1)S(1)} %copy-done, bf16[384,2048]{0,1:T(8,128)(2,1)} %bitcast.64, bf16[2048,2048]{1,0:T(8,128)(2,1)} %all-gather.6.cloned.1.call-done), kind=kOutput, calls=%fused_computation.19 | convolution fusion | flops 3223584768 | bytes 13107200 | tf_op jit(solution)/shard_map/dot_general | solution.py:107
  (146 shorter events, 60.9 us)
Async XLA Ops:
  7.2 10.4 %copy-start = (bf16[384,2048]{1,0:T(8,128)(2,1)S(1)}, bf16[384,2048]{1,0:T(8,128)(2,1)}, u32[]{:S(2)}) copy-start(bf16[384,2048]{1,0:T(8,128)(2,1)} %param.12) | copy-start | bytes 4718596
  7.2 10.8 %copy-start.3 = (bf16[64,128]{1,0:T(8,128)(2,1)S(1)}, bf16[64,128]{1,0:T(8,128)(2,1)}, u32[]{:S(2)}) copy-start(bf16[64,128]{1,0:T(8,128)(2,1)} %param.15) | copy-start | bytes 49156
  7.2 38.4 %copy-start.4 = (bf16[2048]{0:T(1024)(128)(2,1)S(1)}, bf16[2048]{0:T(1024)(128)(2,1)}, u32[]{:S(2)}) copy-start(bf16[2048]{0:T(1024)(128)(2,1)} %param.13) | copy-start | bytes 12292
  8.9 37.4 %all-to-all-start = ((bf16[32,64,128]{2,1,0:T(8,128)(2,1)}), bf16[32,64,128]{2,1,0:T(8,128)(2,1)S(1)}, u32[]{:S(2)}, u32[]{:S(2)}) async-start(bf16[32,64,128]{2,1,0:T(8,128)(2,1)} %tile.2), calls=%async_computation | async-start | bytes 1048576 | tf_op jit(solution)/shard_map/all_to_all | solution.py:15
  17.5 90.1 %all-gather.8.cloned.1.call-start = ((), (), s32[]{:S(2)}) async-start(), calls=%async_computation.3 | async-start | bytes 6488064 | tf_op jit(solution)/shard_map/all_gather | solution.py:127
  46.4 3.0 %copy-start.5 = (s32[96]{0:T(128)S(1)}, s32[96]{0:T(128)}, u32[]{:S(2)}) copy-start(s32[96]{0:T(128)} %param.19) | copy-start | bytes 1156
  46.4 3.8 %copy-start.2 = (s32[12288]{0:T(1024)S(1)}, s32[12288]{0:T(1024)}, u32[]{:S(2)}) copy-start(s32[12288]{0:T(1024)} %param.18) | copy-start | bytes 147460
  47.8 120.0 %all-gather.4.cloned.1.call-start = ((), (), s32[]{:S(2)}) async-start(), calls=%async_computation.1 | async-start | bytes 8650752 | tf_op jit(solution)/shard_map/all_gather | solution.py:69
  48.6 192.7 %all-gather.6.cloned.1.call-start = ((), (), s32[]{:S(2)}) async-start(), calls=%async_computation.2 | async-start | bytes 8650752 | tf_op jit(solution)/shard_map/all_gather | solution.py:109
  52.1 4.8 %collective-permute-start = (bf16[384,256]{0,1:T(8,128)(2,1)}, bf16[384,256]{0,1:T(8,128)(2,1)S(1)}, u32[]{:S(2)}, u32[]{:S(2)}) collective-permute-start(bf16[384,256]{0,1:T(8,128)(2,1)} %pad_maximum_fusion), channel_id=1, source_target_pairs={{0,8},{8,16},{16,24},{24,32},{32,40},{40,48},{48,56},{56,64},{64,7... | collective-permute-start | bytes 589832 | tf_op jit(solution)/shard_map/ppermute | solution.py:21
  56.9 7.4 %collective-permute-start.1 = (bf16[384,256]{0,1:T(8,128)(2,1)S(1)}, bf16[384,256]{0,1:T(8,128)(2,1)S(1)}, u32[]{:S(2)}, u32[]{:S(2)}) collective-permute-start(bf16[384,256]{0,1:T(8,128)(2,1)S(1)} %collective-permute-done), channel_id=1, source_target_pairs={{0,8},{8,16},{16,24},{24,32},{32,40},{40,48},{48,56},{56,64},{64,7... | collective-permute-start | bytes 589832 | tf_op jit(solution)/shard_map/ppermute | solution.py:21
  64.3 8.1 %collective-permute-start.2 = (bf16[384,256]{0,1:T(8,128)(2,1)S(1)}, bf16[384,256]{0,1:T(8,128)(2,1)S(1)}, u32[]{:S(2)}, u32[]{:S(2)}) collective-permute-start(bf16[384,256]{0,1:T(8,128)(2,1)S(1)} %collective-permute-done.1), channel_id=1, source_target_pairs={{0,8},{8,16},{16,24},{24,32},{32,40},{40,48},{48,56},{56,64},{64,7... | collective-permute-start | bytes 589832 | tf_op jit(solution)/shard_map/ppermute | solution.py:21
  177.0 1.0 copy-start.1
  181.1 1.0 copy-start.1
  189.4 1.0 copy-start.1
  197.6 1.0 copy-start.1
  201.7 1.0 copy-start.1
  205.9 1.0 copy-start.1
  210.0 1.0 copy-start.1
  214.2 1.0 copy-start.1
  218.3 1.0 copy-start.1
  222.5 1.0 copy-start.1
  230.8 1.0 copy-start.1
  234.9 1.0 copy-start.1
  (4 other events, 4.0 us)
Sparse Core Ops, SparseCore 0:
  48.0 59.6 all-gather.7
  110.2 57.5 all-gather.3
  170.4 57.5 all-gather.5
